TPU v7x, 32 devices: a whole 2x2x4 slice. The times are simulated.
32 devices in a mesh: rows: 16 (over z, y, x), cols: 2 (over core).
Axes of the slice: x: 2, y: 2, z: 4, core: 2. Of those that a mesh axis runs over, the one named last changes fastest.
Arguments:
- descriptors: bfloat16 [4096, 1024], P(('rows', 'cols')), may hold values from -6 to 6
- sparse_points: bfloat16 [8192, 1024], P('cols'), may hold values from -6 to 6
- point_scale: float32 [8192], P('cols'), may hold values from 0.3 to 3
- env_owner: int32 [4096, 1], P('rows'), may hold values from 0 to 15; in each aligned block of 128 rows (0 to 127, 128 to 255, ...) at most 12 rows name the same one
- env_structure: int32 [4096], P('rows'), may hold values from 0 to 63
- row_weight: float32 [1024], P('rows'), may hold values from 0.01 to 0.1
- ridge_factor: float32 [1], replicated, may hold values from 0.05 to 0.5
Outputs:
- r_rows: float32 [128, 8192], P(None, 'cols')
- reduced: float32 [1024, 8192], P('rows', 'cols')
Inputs may be any that keep to these rules, and one draw needn't show every extreme that they name: `env_owner`: in each aligned block of 128 environments, no owner is named by more than 12 of them.
All inputs are finite; a program needn't handle non-finite values.
Results may differ from a plain program's by a relative error of at most 0.0045.
Values may be sent and summed in bfloat16 or wider, within the bound.
A program may use at most 64 MiB of HBM per device.

v0:
```python
import math

import jax
import jax.numpy as jnp
from jax import lax
from jax.sharding import PartitionSpec as P

PW = 64
PANELS = 2


def from_root(value, axis, source):
    kept = jnp.where(lax.axis_index(axis) == source, value, 0).astype(value.dtype)
    return lax.psum(kept, axis)


def kernel_rows(env_rows, sparse_points, point_scale):
    dot_scale = env_rows.shape[1] ** (-0.5)
    products = (
        lax.dot_general(
            env_rows, sparse_points, (((1,), (1,)), ((), ())), preferred_element_type=jnp.float32
        )
        * dot_scale
    )
    squared = products * products
    return (point_scale[None, :] * squared * squared).astype(jnp.bfloat16)


def pack_slots(kernel, owner_ids, struct_ids, capacity, owner_count):
    row_count = kernel.shape[0]
    labels = lax.broadcasted_iota(jnp.int32, (row_count, owner_count), 1)
    matches = (owner_ids[:, None] == labels).astype(jnp.int32)
    before = jnp.cumsum(matches, axis=0) - matches
    within = jnp.sum(before * matches, axis=1)
    slot_idx = owner_ids * capacity + within
    slot_total = owner_count * capacity
    packed = jnp.zeros((slot_total, kernel.shape[1]), kernel.dtype).at[slot_idx].set(kernel)
    slot_labels = jnp.full((slot_total,), -1, jnp.int32).at[slot_idx].set(struct_ids)
    return (packed, slot_labels)


def fold_structures(received, labels_in, eq_count):
    targets = lax.broadcasted_iota(jnp.int32, (eq_count, labels_in.shape[0]), 0)
    selector = (labels_in[None, :] == targets).astype(jnp.bfloat16)
    return jnp.dot(selector, received, preferred_element_type=jnp.float32)


def inner_cols(left, right):
    return lax.dot_general(
        left,
        right,
        (((0,), (0,)), ((), ())),
        precision=lax.Precision.HIGHEST,
        preferred_element_type=jnp.float32,
    )


def factor(gram_mat, ridge_factor):
    shift = ridge_factor[0] * jnp.trace(gram_mat) / PW + 1e-06
    chol_lower = jnp.linalg.cholesky(gram_mat + shift * jnp.eye(PW, dtype=jnp.float32))
    inverse = jax.scipy.linalg.solve_triangular(
        chol_lower, jnp.eye(PW, dtype=jnp.float32), lower=True
    )
    return (chol_lower, inverse)


def body(
    descriptors, sparse_points, point_scale, env_owner, env_structure, row_weight, ridge_factor
):
    owner_count = lax.axis_size("rows")
    eq_count = row_weight.shape[0]
    owner_ids = env_owner[:, 0]
    env_count = owner_ids.shape[0]
    half_count = env_count // 2
    capacity = max(2, (3 * half_count + 2 * owner_count - 1) // (2 * owner_count))
    kernel_all = kernel_rows(
        lax.all_gather(descriptors, "cols", axis=0, tiled=True), sparse_points, point_scale
    )
    packed, slot_labels = pack_slots(
        kernel_all, owner_ids, env_structure, 2 * capacity, owner_count
    )
    received, labels_in = (
        lax.all_to_all(packed, "rows", split_axis=0, concat_axis=0, tiled=True),
        lax.all_to_all(slot_labels, "rows", split_axis=0, concat_axis=0, tiled=True),
    )
    sums = fold_structures(received, labels_in, eq_count)
    matrix = sums * row_weight[:, None]
    col_count = matrix.shape[1]
    col_ids = lax.axis_index("cols") * col_count + lax.broadcasted_iota(
        jnp.int32, (1, col_count), 1
    )
    norm_scale = 1.0 / math.sqrt(owner_count * eq_count)
    r_blocks = []
    for panel_idx in range(PANELS):
        first_col = panel_idx * PW
        local_cols = lax.slice_in_dim(matrix, first_col, first_col + PW, axis=1)
        panel_cols = from_root(local_cols, "cols", 0)
        gram_mat, cross_terms = lax.psum(
            (inner_cols(panel_cols, panel_cols), inner_cols(panel_cols, matrix)), "rows"
        )
        chol_lower, inverse = factor(gram_mat, ridge_factor)
        q_cols = jnp.dot(
            panel_cols,
            inverse.T,
            precision=lax.Precision.HIGHEST,
            preferred_element_type=jnp.float32,
        )
        coupled = jnp.dot(
            inverse,
            cross_terms,
            precision=lax.Precision.HIGHEST,
            preferred_element_type=jnp.float32,
        )
        later_mask = col_ids >= first_col + PW
        inside = (col_ids >= first_col) & (col_ids < first_col + PW)
        coupled = jnp.where(later_mask, coupled, 0.0)
        update = jnp.dot(
            q_cols, coupled, precision=lax.Precision.HIGHEST, preferred_element_type=jnp.float32
        )
        q_wide = jnp.pad(q_cols, ((0, 0), (first_col, col_count - first_col - PW)))
        matrix = jnp.where(inside, q_wide, matrix - update)
        r_wide = jnp.pad(chol_lower.T, ((0, 0), (first_col, col_count - first_col - PW)))
        r_blocks.append(jnp.where(inside, r_wide, coupled) * norm_scale)
    return (jnp.concatenate(r_blocks, axis=0), matrix)


def solution(mesh):
    return jax.shard_map(
        body,
        mesh=mesh,
        in_specs=(
            P(("rows", "cols"), None),
            P("cols", None),
            P("cols"),
            P("rows", None),
            P("rows"),
            P("rows"),
            P(),
        ),
        out_specs=(P(None, "cols"), P("rows", "cols")),
        check_vma=False,
    )
```

profile of v0, /device:TPU:8, one launch (start us, length us, event | category | flops | bytes accessed | tf_op | source)
XLA Modules:
  0.0 539.4 jit_solution(17488031065577748446)
XLA Ops:
  7.2 0.7 fusion.27
  7.8 0.6 reduce-window.6
  8.4 0.2 slice_reduce_fusion
  8.6 0.8 fusion.19
  9.4 0.7 compare_select_fusion
  10.1 1.6 scatter_custom_fusion
  11.7 0.7 all_to_all.14
  12.4 7.2 %all-to-all-start = ((s32[16,24,1]{1,2,0:T(1,128)}), s32[16,24,1]{1,2,0:T(1,128)S(1)}, u32[]{:S(2)}, u32[]{:S(2)}) async-start(s32[16,24,1]{1,2,0:T(1,128)} %bitcast.5), calls=%async_computation | async-start | bytes 16384 | tf_op jit(solution)/shard_map/all_to_all | solution.py:84
  19.6 2.4 all_gather.3
  22.0 6.0 %fusion.1 = bf16[256,4096]{1,0:T(8,128)(2,1)S(1)} fusion(bf16[256,1024]{1,0:T(8,128)(2,1)S(1)} %all_gather.3, bf16[4096,1024]{1,0:T(8,128)(2,1)} %param.11, f32[4096]{0:T(1024)} %param.12), kind=kOutput, calls=%fused_computation.5 | convolution fusion | flops 2152726528 | bytes 11026432 | tf_op jit(solution)/shard_map/dot_general | solution.py:20
  28.0 5.5 %scatter_custom_fusion.1 = bf16[384,4096]{1,0:T(8,128)(2,1)} fusion(s32[256]{0:T(256)S(1)} %bitcast.82, bf16[256,4096]{1,0:T(8,128)(2,1)S(1)} %fusion.1, bf16[]{:T(256)} %constant.71.clone.1), kind=kCustom, calls=%fused_computation.16 | custom fusion | bytes 3145730 | tf_op jit(solution)/shard_map/scatter | solution.py:37
  33.5 0.0 all-to-all-done
  33.5 0.0 copy-start.4
  33.5 7.0 %all-to-all-start.1 = ((bf16[16,24,4096]{2,1,0:T(8,128)(2,1)}), bf16[16,24,4096]{2,1,0:T(8,128)(2,1)S(1)}, u32[]{:S(2)}, u32[]{:S(2)}) async-start(bf16[16,24,4096]{2,1,0:T(8,128)(2,1)} %bitcast.6), calls=%async_computation.1 | async-start | bytes 6291456 | tf_op jit(solution)/shard_map/all_to_all | solution.py:83
  40.5 0.0 all-reduce.7.cloned.1.call-start
  41.2 0.5 broadcast.141
  41.8 0.7 reduce.9
  42.4 0.1 eq.58
  42.5 66.7 %all-to-all-done.1 = bf16[16,24,4096]{2,1,0:T(8,128)(2,1)S(1)} async-done(((bf16[16,24,4096]{2,1,0:T(8,128)(2,1)}), bf16[16,24,4096]{2,1,0:T(8,128)(2,1)S(1)}, u32[]{:S(2)}, u32[]{:S(2)}) %all-to-all-start.1) | async-done | bytes 3145760 | tf_op jit(solution)/shard_map/all_to_all | solution.py:83
  109.2 1.7 copy-done.2
  110.9 0.0 copy-done.4
  110.9 3.2 convolution_multiply_fusion.1
  114.1 3.4 psum.42
  117.5 0.2 fusion.30
  117.7 3.3 fusion.31
  121.0 71.4 %psum.43 = f32[64,64]{0,1:T(8,128)S(1)} all-reduce(f32[64,64]{0,1:T(8,128)S(1)} %fusion.30), channel_id=1, replica_groups=mesh['rows'=16,'cols'=2] {'rows'}, use_global_device_ids=true, to_apply=%region_6.7 | all-reduce | flops 4096 | bytes 32768 | tf_op jit(solution)/shard_map/psum | solution.py:98
  192.4 0.6 select_reduce_fusion.3
  193.7 0.1 copy.40
  193.8 0.0 all-reduce.7.cloned.1.call-update
  193.8 0.0 all-reduce.9.cloned.1.call-start
  193.9 5.8 %cholesky.44 = f32[64,64]{1,0:T(8,128)S(1)} custom-call(f32[64,64]{1,0:T(8,128)S(1)} %fusion.14), custom_call_target="Cholesky" | custom-call | tf_op jit(solution)/shard_map/jit(cholesky)/cholesky | solution.py:60
  199.8 0.6 compare_reduce_fusion.1
  200.4 0.7 fusion.15
  201.1 4.9 custom-call.6
  206.0 0.3 fusion.9
  206.2 0.2 fusion.32
  206.5 0.1 copy.42
  206.6 101.1 %all-reduce.7.cloned.1.call-done = f32[64,4096]{1,0:T(8,128)} async-done(((f32[64,4096]{1,0:T(8,128)}), f32[64,4096]{1,0:T(8,128)}) %all-reduce.7.cloned.1.call-update) | async-done | bytes 1048592 | tf_op jit(solution)/shard_map/psum | solution.py:98
  307.6 6.5 %select_multiply_fusion.1 = (f32[64,4096]{0,1:T(8,128)}, f32[64,4096]{0,1:T(8,128)S(1)}) fusion(f32[64,64]{0,1:T(8,128)S(1)} %get-tuple-element.10, pred[4096]{0:T(1024)(128)(4,1)S(1)} %get-tuple-element.21, f32[64,64]{1,0:T(8,128)S(1)} %fusion.9, f32[64,4096]{1,0:T(8,128)} %all-reduce.7.cloned.1.call-done, pred[4096]{0:T(1024)(128)(4,1)S(1)} %get-tuple-element.20), kind=kOutput, calls=%fused_computation.15 | convolution fusion | flops 202113024 | bytes 3186688 | tf_op jit(solution)/shard_map/dot_general | solution.py:108
  314.1 2.0 fusion.3
  316.1 0.0 copy-start
  316.1 1.3 copy-done
  317.5 3.4 psum.45
  320.9 0.2 fusion.33
  321.1 4.9 fusion.34
  325.9 69.5 %psum.46 = f32[64,64]{0,1:T(8,128)S(1)} all-reduce(f32[64,64]{0,1:T(8,128)S(1)} %fusion.33), channel_id=1, replica_groups=mesh['rows'=16,'cols'=2] {'rows'}, use_global_device_ids=true, to_apply=%region_12.15 | all-reduce | flops 4096 | bytes 32768 | tf_op jit(solution)/shard_map/psum | solution.py:98
  395.5 0.6 select_reduce_fusion.2
  396.7 0.1 copy.45
  396.8 0.0 all-reduce.9.cloned.1.call-update
  396.9 5.8 %cholesky.55 = f32[64,64]{1,0:T(8,128)S(1)} custom-call(f32[64,64]{1,0:T(8,128)S(1)} %fusion.12), custom_call_target="Cholesky" | custom-call | tf_op jit(solution)/shard_map/jit(cholesky)/cholesky | solution.py:60
  402.8 0.7 compare_reduce_fusion
  403.4 0.6 fusion.16
  404.0 4.9 custom-call.7
  408.9 0.3 fusion.7
  409.2 0.2 fusion.35
  409.4 0.1 copy.47
  409.5 101.2 %all-reduce.9.cloned.1.call-done = f32[64,4096]{1,0:T(8,128)} async-done(((f32[64,4096]{1,0:T(8,128)}), f32[64,4096]{1,0:T(8,128)}) %all-reduce.9.cloned.1.call-update) | async-done | bytes 1048592 | tf_op jit(solution)/shard_map/psum | solution.py:98
  510.7 6.7 %select_multiply_fusion = (f32[64,4096]{0,1:T(8,128)}, f32[64,4096]{0,1:T(8,128)S(1)}) fusion(f32[64,64]{0,1:T(8,128)S(1)} %get-tuple-element.12, pred[4096]{0:T(1024)(128)(4,1)S(1)} %get-tuple-element.19, f32[64,64]{1,0:T(8,128)S(1)} %fusion.7, f32[64,4096]{1,0:T(8,128)} %all-reduce.9.cloned.1.call-done, pred[4096]{0:T(1024)(128)(4,1)S(1)} %get-tuple-element.18), kind=kOutput, calls=%fused_computation.14 | convolution fusion | flops 202113024 | bytes 3186688 | tf_op jit(solution)/shard_map/dot_general | solution.py:108
  517.4 0.0 copy-done.1
  517.4 5.4 %fusion.2 = f32[64,4096]{0,1:T(8,128)} fusion(f32[64,4096]{0,1:T(8,128)S(1)} %copy-done.1, f32[64,64]{1,0:T(8,128)S(1)} %fusion.35, f32[64,4096]{0,1:T(8,128)S(1)} %get-tuple-element.15, f32[64,64]{0,1:T(8,128)S(1)} %copy.47, pred[4096]{0:T(1024)(128)(4,1)S(1)} %get-tuple-element.19), kind=kOutput, calls=%fused_computation.9 | convolution fusion | flops 201850880 | bytes 3182592 | tf_op jit(solution)/shard_map/dot_general | solution.py:117
  522.8 3.3 copy.50
  526.1 0.0 copy-done.3
  526.1 3.6 pad_maximum_fusion
  529.7 2.9 copy.49
  (15 shorter events, 0.2 us)
Async XLA Ops:
  12.4 21.1 %all-to-all-start = ((s32[16,24,1]{1,2,0:T(1,128)}), s32[16,24,1]{1,2,0:T(1,128)S(1)}, u32[]{:S(2)}, u32[]{:S(2)}) async-start(s32[16,24,1]{1,2,0:T(1,128)} %bitcast.5), calls=%async_computation | async-start | bytes 16384 | tf_op jit(solution)/shard_map/all_to_all | solution.py:84
  33.5 77.4 %copy-start.4 = (f32[64]{0:T(128)S(1)}, f32[64]{0:T(128)}, u32[]{:S(2)}) copy-start(f32[64]{0:T(128)} %param.15) | copy-start | bytes 772
  33.5 75.7 %all-to-all-start.1 = ((bf16[16,24,4096]{2,1,0:T(8,128)(2,1)}), bf16[16,24,4096]{2,1,0:T(8,128)(2,1)S(1)}, u32[]{:S(2)}, u32[]{:S(2)}) async-start(bf16[16,24,4096]{2,1,0:T(8,128)(2,1)} %bitcast.6), calls=%async_computation.1 | async-start | bytes 6291456 | tf_op jit(solution)/shard_map/all_to_all | solution.py:83
  40.5 267.1 %all-reduce.7.cloned.1.call-start = ((), (), s32[]{:S(2)}) async-start(), calls=%async_computation.2 | async-start | bytes 2097152 | tf_op jit(solution)/shard_map/psum | solution.py:98
  109.2 1.7 copy-start.2
  193.8 316.9 %all-reduce.9.cloned.1.call-start = ((), (), s32[]{:S(2)}) async-start(), calls=%async_computation.3 | async-start | bytes 2097152 | tf_op jit(solution)/shard_map/psum | solution.py:98
  316.1 1.4 copy-start
  510.7 6.7 %copy-start.1 = (f32[64,4096]{0,1:T(8,128)S(1)}, f32[64,4096]{0,1:T(8,128)}, u32[]{:S(2)}) copy-start(f32[64,4096]{0,1:T(8,128)} %copy-done) | copy-start | bytes 3145732
  522.8 3.3 copy-start.3
Sparse Core Ops, SparseCore 0:
  193.9 113.6 all-reduce.6
  397.0 113.6 all-reduce.8
where the time goes:
time: 542 us; the launch traced here: 539 us
  waiting for transfers between devices  269 us (50%)
  blocking collectives  150 us (28%)
  matrix products  39.3 us (7%)
  other arithmetic  32.4 us (6%)
  local copies, waits for them, and re-layouts  18 us (3%)
  between operations  16.2 us (3%)
  starting transfers between devices  14.4 us (3%)
    psum x2, waiting for transfers between devices, body(): lax.psum((inner_cols(panel_cols, panel_cols), inner_cols(panel_cols, matr...  202 us
    psum x2, blocking collectives, body(): lax.psum((inner_cols(panel_cols, panel_cols), inner_cols(panel_cols, matr...  141 us
    all_to_all x1, waiting for transfers between devices, body(): lax.all_to_all(packed, 'rows', split_axis=0, concat_axis=0, tiled=True)  66.7 us
    dot_general x2, matrix products, body(): jnp.dot(inverse, cross_terms, precision=lax.Precision.HIGHEST, preferred_...  13.2 us
    another operation x6, other arithmetic, factor(): jnp.linalg.cholesky(gram_mat + shift * jnp.eye(PW, dtype=jnp.float32))  13 us
  transfers between devices with their start and end apart: 4, of which 3 were waited for; matrix products, arithmetic and copies ran while one was open for 7% of the time, Pallas kernels for 0%

commit v1 on v0

v1 whole, which is shorter than its diff:
```python
import math

import jax
import jax.numpy as jnp
from jax import lax
from jax.sharding import PartitionSpec as P

PW = 64
PANELS = 2
BLOCK = 128
LANES = 128
HI = lax.Precision.HIGHEST
F32 = jnp.float32


def mm(left, right, contract, precision=HI):
    return lax.dot_general(
        left, right, ((contract[0], contract[1]), ((), ())), precision=precision,
        preferred_element_type=F32,
    )


def from_root(value, axis):
    return lax.all_gather(value, axis)[0]


def kernel_rows(env_rows, points, scale):
    products = mm(env_rows, points, ((1,), (1,)), None) * env_rows.shape[1] ** (-0.5)
    squared = products * products
    return (scale[None, :] * squared * squared).astype(jnp.bfloat16)


def spread(value, axis):
    size = lax.axis_size(axis)
    return lax.all_to_all(
        jnp.broadcast_to(value[None], (size,) + value.shape), axis, 0, 0, tiled=True
    )


def factor(gram_mat, ridge_factor):
    eye = jnp.eye(PW, dtype=F32)
    shift = ridge_factor[0] * jnp.trace(gram_mat) / PW + 1e-06
    chol_lower = jnp.linalg.cholesky(gram_mat + shift * eye)
    return chol_lower, jax.scipy.linalg.solve_triangular(chol_lower, eye, lower=True)


def body(
    descriptors, sparse_points, point_scale, env_owner, env_structure, row_weight, ridge_factor
):
    owners = lax.axis_size("rows")
    col_index = lax.axis_index("cols")
    eq_count = row_weight.shape[0]
    env_local, desc = descriptors.shape
    wide = PANELS * PW

    head_points = from_root(sparse_points[:wide], "cols")
    head_scale = from_root(point_scale[:wide], "cols")

    per_block = max(2, (3 * BLOCK + 2 * owners - 1) // (2 * owners))
    capacity = min(env_local, per_block * (-(-env_local // BLOCK)))
    own = lax.dynamic_slice_in_dim(env_owner[:, 0], col_index * env_local, env_local)
    struct = lax.dynamic_slice_in_dim(env_structure, col_index * env_local, env_local)
    idx = jnp.arange(env_local)
    within = jnp.sum(
        ((own[:, None] == own[None, :]) & (idx[None, :] < idx[:, None])).astype(jnp.int32), axis=1
    )
    slot = own * capacity + within
    slots = lax.broadcasted_iota(jnp.int32, (owners * capacity, env_local), 0)
    pick = (slots == slot[None, :]).astype(jnp.bfloat16)
    lane = lax.broadcasted_iota(jnp.int32, (env_local, LANES), 1)
    tag = jnp.where(lane == 0, struct[:, None] + 1, 0).astype(jnp.bfloat16)
    payload = mm(
        pick, jnp.concatenate([descriptors, tag], axis=1), ((1,), (0,)), None
    ).astype(jnp.bfloat16)
    arrived = lax.all_to_all(payload, "rows", 0, 0, tiled=True)
    arrived = lax.all_gather(arrived, "cols", axis=0, tiled=True)
    env_rows = arrived[:, :desc]
    labels = arrived[:, desc].astype(jnp.int32) - 1
    targets = lax.broadcasted_iota(jnp.int32, (eq_count, labels.shape[0]), 0)
    selector = (labels[None, :] == targets).astype(jnp.bfloat16)

    def equations(points, scale):
        kernel = kernel_rows(env_rows, points, scale)
        return mm(selector, kernel, ((1,), (0,)), None) * row_weight[:, None]

    head = equations(head_points, head_scale)
    head_all = spread(head, "rows").reshape(owners * eq_count, wide)
    matrix = equations(sparse_points, point_scale)
    col_count = matrix.shape[1]

    part = col_count // owners
    cross = mm(head, matrix, ((0,), (0,)))
    cross = cross.reshape(wide, owners, part).transpose(1, 0, 2).astype(jnp.bfloat16)
    cross = lax.all_to_all(cross, "rows", 0, 0, tiled=True)
    cross = jnp.sum(cross.astype(F32), axis=0)

    gram = mm(head_all, head_all, ((0,), (0,)))
    low1, inv1 = factor(gram[:PW, :PW], ridge_factor)
    c12 = mm(inv1, gram[:PW, PW:], ((1,), (0,)))
    overlap = mm(mm(inv1, gram[:PW, :PW], ((1,), (0,))), inv1, ((1,), (1,)))
    twice = 2.0 * jnp.eye(PW, dtype=F32) - overlap
    mixed = mm(c12, twice, ((0,), (0,)))
    low2, inv2 = factor(gram[PW:, PW:] - mm(mixed, c12, ((1,), (0,))), ridge_factor)
    q1 = mm(head[:, :PW], inv1, ((1,), (1,)))
    q2 = mm(head[:, PW:] - mm(q1, c12, ((1,), (0,))), inv2, ((1,), (1,)))

    c1 = mm(inv1, cross[:PW], ((1,), (0,)))
    c2 = mm(inv2, cross[PW:] - mm(mixed, c1, ((1,), (0,))), ((1,), (0,)))
    coupled = spread(jnp.concatenate([c1, c2], axis=0).astype(jnp.bfloat16), "rows")
    coupled = coupled.transpose(1, 0, 2).reshape(wide, col_count).astype(F32)

    q_cols = jnp.concatenate([q1, q2], axis=1)
    update = mm(q_cols, coupled, ((1,), (0,)))
    norm_scale = 1.0 / math.sqrt(owners * eq_count)
    zero = jnp.zeros((PW, PW), F32)
    r_head = jnp.concatenate(
        [jnp.concatenate([low1.T, c12], axis=1), jnp.concatenate([zero, low2.T], axis=1)], axis=0
    )
    root = col_index == 0
    reduced = matrix - update
    reduced_head = jnp.where(root, q_cols, reduced[:, :wide])
    r_head = jnp.where(root, r_head, coupled[:, :wide])
    reduced = jnp.concatenate([reduced_head, reduced[:, wide:]], axis=1)
    r_rows = jnp.concatenate([r_head, coupled[:, wide:]], axis=1) * norm_scale
    return r_rows, reduced


def solution(mesh):
    return jax.shard_map(
        body,
        mesh=mesh,
        in_specs=(
            P(("rows", "cols"), None),
            P("cols", None),
            P("cols"),
            P("rows", None),
            P("rows"),
            P("rows"),
            P(),
        ),
        out_specs=(P(None, "cols"), P("rows", "cols")),
        check_vma=False,
    )
```

time: 542 us -> 125 us (0.23)
  waiting for transfers between devices: 269 us -> 40.2 us
  blocking collectives: 150 us -> 6.42 us
  matrix products: 39.3 us -> 15.6 us
  between operations: 16.2 us -> 2.94 us
  local copies, waits for them, and re-layouts: 18 us -> 7.85 us
  starting transfers between devices: 14.4 us -> 23.3 us
    psum x2 -> x0, waiting for transfers between devices: 202 us -> none  [body(): lax.psum((inner_cols(panel_cols, panel_cols), inner_cols(panel_cols, matr...]
    psum x4 -> x0, blocking collectives: 148 us -> none  [the longest x2 141 us: body(): lax.psum((inner_cols(panel_cols, panel_cols), inner_cols(panel_cols, matr...]
    all_to_all x2 -> x4, waiting for transfers between devices: 66.7 us -> 40.2 us  [the longest x2 29 us: spread(): lax.all_to_all(jnp.broadcast_to(value[None], (size,) + value.shape), axis...]
    dot_general x12 -> x17, matrix products: 38.8 us -> 15.1 us  [mm(): lax.dot_general(left, right, ((contract[0], contract[1]), ((), ())), prec...]
    all_to_all x2 -> x4, starting transfers between devices: 14.3 us -> 23.3 us  [the longest x2 11.5 us: spread(): lax.all_to_all(jnp.broadcast_to(value[None], (size,) + value.shape), axis...]
    scatter x2 -> x0, local copies, waits for them, and re-layouts: 7.04 us -> none  [the longest x1 5.49 us: pack_slots(): jnp.zeros((slot_total, kernel.shape[1]), kernel.dtype).at[slot_idx]]
    unnamed x12 -> x11, local copies, waits for them, and re-layouts: 9.2 us -> 2.6 us
    another operation x10 -> x8, other arithmetic: 23.4 us -> 22.8 us  [the longest x6 13 us: factor(): chol_lower = jnp.linalg.cholesky(gram_mat + shift * eye)]
  transfers between devices with their start and end apart: 4 -> 4, of which waited for: 3 -> 3; matrix products, arithmetic and copies ran while one was open for 7% -> 31% of each run, Pallas kernels for 0% -> 0%
where the time goes in v1:
time: 125 us
  waiting for transfers between devices  40.2 us (32%)
  other arithmetic  28.4 us (23%)
  starting transfers between devices  23.3 us (19%)
  matrix products  15.6 us (12%)
  local copies, waits for them, and re-layouts  7.85 us (6%)
  blocking collectives  6.42 us (5%)
  between operations  2.94 us (2%)
    all_to_all x2, waiting for transfers between devices, spread(): lax.all_to_all(jnp.broadcast_to(value[None], (size,) + value.shape), axis...  29 us
    dot_general x17, matrix products, mm(): lax.dot_general(left, right, ((contract[0], contract[1]), ((), ())), prec...  15.1 us
    another operation x6, other arithmetic, factor(): chol_lower = jnp.linalg.cholesky(gram_mat + shift * eye)  13 us
    all_to_all x2, starting transfers between devices, spread(): lax.all_to_all(jnp.broadcast_to(value[None], (size,) + value.shape), axis...  11.5 us
    all_to_all x1, waiting for transfers between devices, body(): arrived = lax.all_to_all(payload, 'rows', 0, 0, tiled=True)  11.2 us
    another operation x2, other arithmetic, factor(): jax.scipy.linalg.solve_triangular(chol_lower, eye, lower=True)  9.79 us
    all_to_all x1, starting transfers between devices, body(): arrived = lax.all_to_all(payload, 'rows', 0, 0, tiled=True)  7.22 us
    all_to_all x1, starting transfers between devices, body(): cross = lax.all_to_all(cross, 'rows', 0, 0, tiled=True)  4.56 us
  transfers between devices with their start and end apart: 4, of which 3 were waited for; matrix products, arithmetic and copies ran while one was open for 31% of the time, Pallas kernels for 0%

profile of v1, /device:TPU:8, one launch (start us, length us, event | category | flops | bytes accessed | tf_op | source)
XLA Modules:
  0.0 124.6 jit_solution(13761255748347640097)
XLA Ops:
  0.7 0.8 dynamic-slice_add_fusion
  1.5 0.7 dynamic-slice_bitcast_fusion
  2.1 0.2 convert_reduce_fusion.1
  2.3 0.7 multiply_add_fusion
  3.0 0.1 select_convert_fusion
  3.1 1.2 convolution_convert_fusion.1
  4.3 0.9 all_to_all.17
  5.2 7.2 %all-to-all-start = ((bf16[16,12,1152]{2,1,0:T(8,128)(2,1)}), bf16[16,12,1152]{2,1,0:T(8,128)(2,1)S(1)}, u32[]{:S(2)}, u32[]{:S(2)}) async-start(bf16[16,12,1152]{2,1,0:T(8,128)(2,1)} %all_to_all.17), calls=%async_computation | async-start | bytes 1179648 | tf_op jit(solution)/shard_map/all_to_all | solution.py:75
  13.1 1.8 %all-gather.2 = f32[2,1,128]{2,1,0:T(1,128)S(1)} all-gather(f32[1,1,128]{2,1,0:T(1,128)S(1)} %slice_bitcast_fusion.1), channel_id=2, replica_groups=mesh['rows'=16,'cols'=2] {'cols'}, dimensions={0}, use_global_device_ids=true | all-gather | bytes 1536 | tf_op jit(solution)/shard_map/all_gather | solution.py:24
  14.9 2.2 %all-gather.1 = bf16[256,1024]{1,0:T(8,128)(2,1)S(1)} all-gather(bf16[128,1024]{1,0:T(8,128)(2,1)S(1)} %slice-done.1), channel_id=3, replica_groups=mesh['rows'=16,'cols'=2] {'cols'}, dimensions={0}, use_global_device_ids=true | all-gather | bytes 786432 | tf_op jit(solution)/shard_map/all_gather | solution.py:24
  17.1 11.2 %all-to-all-done = bf16[16,12,1152]{2,1,0:T(8,128)(2,1)S(1)} async-done(((bf16[16,12,1152]{2,1,0:T(8,128)(2,1)}), bf16[16,12,1152]{2,1,0:T(8,128)(2,1)S(1)}, u32[]{:S(2)}, u32[]{:S(2)}) %all-to-all-start) | async-done | bytes 442400 | tf_op jit(solution)/shard_map/all_to_all | solution.py:75
  28.3 0.1 all_to_all.19
  28.4 2.4 %all_gather.15 = bf16[384,1152]{1,0:T(8,128)(2,1)S(1)} all-gather(bf16[192,1152]{1,0:T(8,128)(2,1)S(1)} %all_to_all.19), channel_id=1, replica_groups=mesh['rows'=16,'cols'=2] {'cols'}, dimensions={0}, use_global_device_ids=true | all-gather | bytes 1327104 | tf_op jit(solution)/shard_map/all_gather | solution.py:76
  30.8 0.1 add_reduce_fusion
  31.0 0.5 convolution_multiply_fusion.2
  31.5 0.8 broadcast_in_dim.19
  32.3 4.6 %all-to-all-start.1 = ((f32[16,64,128]{2,1,0:T(8,128)}), f32[16,64,128]{2,1,0:T(8,128)S(1)}, u32[]{:S(2)}, u32[]{:S(2)}) async-start(f32[16,64,128]{2,1,0:T(8,128)} %broadcast_in_dim.19), calls=%async_computation.1 | async-start | bytes 1048576 | tf_op jit(solution)/shard_map/all_to_all | solution.py:35
  37.0 6.5 %convolution_multiply_fusion = f32[64,4096]{1,0:T(8,128)S(1)} fusion(bf16[4096,1024]{1,0:T(8,128)(2,1)} %param.11, f32[4096]{0:T(1024)S(1)} %copy-done.1, bf16[384,1152]{1,0:T(8,128)(2,1)S(1)} %all_gather.15, f32[64]{0:T(128)S(1)} %copy-done.2, s32[384]{0:T(512)S(1)} %add_reduce_fusion), kind=kOutput, calls=%fused_computation.4 | convolution fusion | flops 3430703104 | bytes 10242560 | tf_op jit(solution)/shard_map/dot_general | solution.py:17
  43.4 1.8 %convolution_convert_fusion = bf16[128,4096]{1,0:T(8,128)(2,1)S(1)} fusion(f32[64,128]{1,0:T(8,128)S(1)} %convolution_multiply_fusion.2, f32[64,4096]{1,0:T(8,128)S(1)} %convolution_multiply_fusion), kind=kOutput, calls=%fused_computation.2 | convolution fusion | flops 403177472 | bytes 2129920 | tf_op jit(solution)/shard_map/dot_general | solution.py:17
  45.3 1.1 copy.51
  46.3 5.4 %all-to-all-done.1 = f32[16,64,128]{2,1,0:T(8,128)S(1)} async-done(((f32[16,64,128]{2,1,0:T(8,128)}), f32[16,64,128]{2,1,0:T(8,128)S(1)}, u32[]{:S(2)}, u32[]{:S(2)}) %all-to-all-start.1) | async-done | bytes 524320 | tf_op jit(solution)/shard_map/all_to_all | solution.py:35
  51.7 4.6 %all-to-all-start.2 = ((bf16[16,128,256]{2,1,0:T(8,128)(2,1)}), bf16[16,128,256]{2,1,0:T(8,128)(2,1)S(1)}, u32[]{:S(2)}, u32[]{:S(2)}) async-start(bf16[16,128,256]{2,1,0:T(8,128)(2,1)} %bitcast.67), calls=%async_computation.2 | async-start | bytes 2097152 | tf_op jit(solution)/shard_map/all_to_all | solution.py:94
  56.3 1.0 convolution_bitcast_fusion
  57.3 0.1 fusion.45
  57.4 0.1 copy.47
  57.5 0.6 select_reduce_fusion.3
  58.8 0.1 copy.36
  58.9 5.8 %cholesky.44 = f32[64,64]{1,0:T(8,128)S(1)} custom-call(f32[64,64]{1,0:T(8,128)S(1)} %fusion.36), custom_call_target="Cholesky" | custom-call | tf_op jit(solution)/shard_map/jit(cholesky)/cholesky | solution.py:43
  64.7 0.6 compare_reduce_fusion.1
  65.4 0.7 fusion.37
  66.0 4.9 %custom-call.6 = f32[1,64,64]{1,2,0:T(8,128)S(1)} custom-call(f32[1,64,64]{2,1,0:T(8,128)S(1)} %get-tuple-element.15), custom_call_target="InvertDiagBlocksLowerTriangular" | custom-call | tf_op jit(solution)/shard_map/jit(_solve_triangular)/triangular_solve | solution.py:44
  70.9 0.3 fusion.27
  71.2 0.2 fusion.31
  71.4 0.1 copy.48
  71.5 0.2 fusion.43
  71.7 0.2 convolution_subtract_fusion.4
  71.9 0.2 fusion.47
  72.1 0.8 select_reduce_fusion.2
  73.6 0.1 copy.41
  73.7 5.8 %cholesky.55 = f32[64,64]{1,0:T(8,128)S(1)} custom-call(f32[64,64]{1,0:T(8,128)S(1)} %fusion.34), custom_call_target="Cholesky" | custom-call | tf_op jit(solution)/shard_map/jit(cholesky)/cholesky | solution.py:43
  79.6 0.6 compare_reduce_fusion
  80.3 0.7 fusion.38
  80.9 4.9 %custom-call.7 = f32[1,64,64]{1,2,0:T(8,128)S(1)} custom-call(f32[1,64,64]{2,1,0:T(8,128)S(1)} %get-tuple-element.17), custom_call_target="InvertDiagBlocksLowerTriangular" | custom-call | tf_op jit(solution)/shard_map/jit(_solve_triangular)/triangular_solve | solution.py:44
  85.8 0.3 fusion.25
  86.1 0.1 convert_reduce_fusion
  86.2 0.2 fusion.46
  86.4 0.2 convolution_subtract_fusion.1
  86.6 0.2 convolution_convert_fusion.2
  86.9 0.1 copy.43
  87.0 1.2 broadcast_in_dim.21
  88.2 6.9 %all-to-all-start.3 = ((bf16[16,128,256]{1,2,0:T(8,128)(2,1)}), bf16[16,128,256]{1,2,0:T(8,128)(2,1)S(1)}, u32[]{:S(2)}, u32[]{:S(2)}) async-start(bf16[16,128,256]{1,2,0:T(8,128)(2,1)} %broadcast_in_dim.21), calls=%async_computation.3 | async-start | bytes 2097152 | tf_op jit(solution)/shard_map/all_to_all | solution.py:35
  95.1 0.2 fusion.29
  95.3 0.2 convolution_subtract_fusion.2
  95.5 0.2 fusion.48
  95.7 23.6 %all-to-all-done.3 = bf16[16,128,256]{1,2,0:T(8,128)(2,1)S(1)} async-done(((bf16[16,128,256]{1,2,0:T(8,128)(2,1)}), bf16[16,128,256]{1,2,0:T(8,128)(2,1)S(1)}, u32[]{:S(2)}, u32[]{:S(2)}) %all-to-all-start.3) | async-done | bytes 1048608 | tf_op jit(solution)/shard_map/all_to_all | solution.py:35
  119.3 1.2 convolution_subtract_fusion
  120.6 0.1 slice_select_fusion.1
  120.7 0.2 bitcast_convert_fusion
  120.9 0.1 slice.90
  121.0 0.5 copy-done
  121.6 0.1 slice_select_fusion
  121.6 0.1 maximum_multiply_fusion
  121.8 1.8 %copy.44 = f32[128,4096]{1,0:T(8,128)} copy(f32[128,4096]{0,1:T(8,128)S(1)} %maximum_multiply_fusion) | data formatting | bytes 4194304
  123.6 1.0 pad_maximum_fusion
  (21 shorter events, 0.2 us)
Async XLA Ops:
  0.6 14.3 %slice-start.1 = ((bf16[4096,1024]{1,0:T(8,128)(2,1)}), bf16[128,1024]{1,0:T(8,128)(2,1)S(1)}, s32[]{:S(2)}) async-start(bf16[4096,1024]{1,0:T(8,128)(2,1)} %param.11), calls=%async_computation.5 | async-start | bytes 524288 | tf_op jit(solution)/shard_map/slice | solution.py:56
  0.6 12.4 %copy-start.1 = (f32[4096]{0:T(1024)S(1)}, f32[4096]{0:T(1024)}, u32[]{:S(2)}) copy-start(f32[4096]{0:T(1024)} %param.12) | copy-start | bytes 49156
  4.3 26.7 %copy-start.2 = (f32[64]{0:T(128)S(1)}, f32[64]{0:T(128)}, u32[]{:S(2)}) copy-start(f32[64]{0:T(128)} %param.15) | copy-start | bytes 772
  5.2 23.1 %all-to-all-start = ((bf16[16,12,1152]{2,1,0:T(8,128)(2,1)}), bf16[16,12,1152]{2,1,0:T(8,128)(2,1)S(1)}, u32[]{:S(2)}, u32[]{:S(2)}) async-start(bf16[16,12,1152]{2,1,0:T(8,128)(2,1)} %all_to_all.17), calls=%async_computation | async-start | bytes 1179648 | tf_op jit(solution)/shard_map/all_to_all | solution.py:75
  32.3 19.4 %all-to-all-start.1 = ((f32[16,64,128]{2,1,0:T(8,128)}), f32[16,64,128]{2,1,0:T(8,128)S(1)}, u32[]{:S(2)}, u32[]{:S(2)}) async-start(f32[16,64,128]{2,1,0:T(8,128)} %broadcast_in_dim.19), calls=%async_computation.1 | async-start | bytes 1048576 | tf_op jit(solution)/shard_map/all_to_all | solution.py:35
  51.7 34.3 %all-to-all-start.2 = ((bf16[16,128,256]{2,1,0:T(8,128)(2,1)}), bf16[16,128,256]{2,1,0:T(8,128)(2,1)S(1)}, u32[]{:S(2)}, u32[]{:S(2)}) async-start(bf16[16,128,256]{2,1,0:T(8,128)(2,1)} %bitcast.67), calls=%async_computation.2 | async-start | bytes 2097152 | tf_op jit(solution)/shard_map/all_to_all | solution.py:94
  88.2 31.2 %all-to-all-start.3 = ((bf16[16,128,256]{1,2,0:T(8,128)(2,1)}), bf16[16,128,256]{1,2,0:T(8,128)(2,1)S(1)}, u32[]{:S(2)}, u32[]{:S(2)}) async-start(bf16[16,128,256]{1,2,0:T(8,128)(2,1)} %broadcast_in_dim.21), calls=%async_computation.3 | async-start | bytes 2097152 | tf_op jit(solution)/shard_map/all_to_all | solution.py:35
  120.6 1.0 copy-start
  121.8 1.8 %slice-start = ((f32[64,4096]{1,0:T(8,128)}), f32[64,3968]{1,0:T(8,128)S(1)}, s32[]{:S(2)}) async-start(f32[64,4096]{1,0:T(8,128)} %copy-done), calls=%async_computation.4 | async-start | bytes 2031616 | tf_op jit(solution)/shard_map/slice | solution.py:123

commit v2 on v1

--- a/solution.py
+++ b/solution.py
@@ -3,6 +3,8 @@
 import jax
 import jax.numpy as jnp
 from jax import lax
+from jax.experimental import pallas as pl
+from jax.experimental.pallas import tpu as pltpu
 from jax.sharding import PartitionSpec as P
 
 PW = 64
@@ -37,11 +39,28 @@
     )
 
 
+def eliminate(in_ref, out_ref):
+    work = in_ref[...]
+    rows = lax.broadcasted_iota(jnp.int32, work.shape, 0)
+    lanes = lax.broadcasted_iota(jnp.int32, work.shape, 1)
+    for k in range(PW):
+        ratio = work[:, k : k + 1] / work[k : k + 1, k : k + 1]
+        work = work - jnp.where(rows > k, ratio * work[k : k + 1, :], 0.0)
+    pivots = jnp.sum(jnp.where(lanes == rows, work, 0.0), axis=1, keepdims=True)
+    out_ref[...] = jnp.where(lanes < rows, 0.0, work / jnp.sqrt(pivots))
+
+
 def factor(gram_mat, ridge_factor):
     eye = jnp.eye(PW, dtype=F32)
     shift = ridge_factor[0] * jnp.trace(gram_mat) / PW + 1e-06
-    chol_lower = jnp.linalg.cholesky(gram_mat + shift * eye)
-    return chol_lower, jax.scipy.linalg.solve_triangular(chol_lower, eye, lower=True)
+    both = pl.pallas_call(
+        eliminate,
+        out_shape=jax.ShapeDtypeStruct((PW, 2 * PW), F32),
+        in_specs=[pl.BlockSpec(memory_space=pltpu.VMEM)],
+        out_specs=pl.BlockSpec(memory_space=pltpu.VMEM),
+        cost_estimate=pl.CostEstimate(flops=8000000, bytes_accessed=65536, transcendentals=0),
+    )(jnp.concatenate([gram_mat + shift * eye, eye], axis=1))
+    return both[:, :PW], both[:, PW:]
 
 
 def body(
@@ -89,18 +108,26 @@
     col_count = matrix.shape[1]
 
     part = col_count // owners
-    cross = mm(head, matrix, ((0,), (0,)))
-    cross = cross.reshape(wide, owners, part).transpose(1, 0, 2).astype(jnp.bfloat16)
-    cross = lax.all_to_all(cross, "rows", 0, 0, tiled=True)
-    cross = jnp.sum(cross.astype(F32), axis=0)
+    level = head_scale / jnp.sum(head_scale * head_scale)
+    along = jnp.sum(head * level[None, :], axis=1, keepdims=True)
+    rest = head - along * head_scale[None, :]
+    cross = mm(rest, matrix, ((0,), (0,)))
+    lead = mm(along, matrix, ((0,), (0,)))
+    lead_top = lax.reduce_precision(lead, 8, 7)
+    pad = jnp.zeros((14, col_count), F32)
+    sent = jnp.concatenate([cross, lead_top, lead - lead_top, pad], axis=0)
+    sent = sent.reshape(wide + 16, owners, part).transpose(1, 0, 2).astype(jnp.bfloat16)
+    sent = lax.all_to_all(sent, "rows", 0, 0, tiled=True)
+    sent = jnp.sum(sent.astype(F32), axis=0)
+    cross = sent[:wide] + head_scale[:, None] * (sent[wide] + sent[wide + 1])[None, :]
 
     gram = mm(head_all, head_all, ((0,), (0,)))
-    low1, inv1 = factor(gram[:PW, :PW], ridge_factor)
+    up1, inv1 = factor(gram[:PW, :PW], ridge_factor)
     c12 = mm(inv1, gram[:PW, PW:], ((1,), (0,)))
     overlap = mm(mm(inv1, gram[:PW, :PW], ((1,), (0,))), inv1, ((1,), (1,)))
     twice = 2.0 * jnp.eye(PW, dtype=F32) - overlap
     mixed = mm(c12, twice, ((0,), (0,)))
-    low2, inv2 = factor(gram[PW:, PW:] - mm(mixed, c12, ((1,), (0,))), ridge_factor)
+    up2, inv2 = factor(gram[PW:, PW:] - mm(mixed, c12, ((1,), (0,))), ridge_factor)
     q1 = mm(head[:, :PW], inv1, ((1,), (1,)))
     q2 = mm(head[:, PW:] - mm(q1, c12, ((1,), (0,))), inv2, ((1,), (1,)))
 
@@ -114,7 +141,7 @@
     norm_scale = 1.0 / math.sqrt(owners * eq_count)
     zero = jnp.zeros((PW, PW), F32)
     r_head = jnp.concatenate(
-        [jnp.concatenate([low1.T, c12], axis=1), jnp.concatenate([zero, low2.T], axis=1)], axis=0
+        [jnp.concatenate([up1, c12], axis=1), jnp.concatenate([zero, up2], axis=1)], axis=0
     )
     root = col_index == 0
     reduced = matrix - update

time: 125 us -> 128 us (1.024)
  other arithmetic: 28.4 us -> 9.8 us
  Pallas kernels: 0 us -> 13.3 us
  waiting for transfers between devices: 40.2 us -> 50.1 us
  local copies, waits for them, and re-layouts: 7.85 us -> 4.16 us
  matrix products: 15.6 us -> 18.7 us
  starting transfers between devices: 23.3 us -> 21.1 us
    another operation x8 -> x1, other arithmetic: 22.8 us -> 0.01 us  [the longest x6 13 us: factor(): chol_lower = jnp.linalg.cholesky(gram_mat + shift * eye)]
    pallas_call x0 -> x2, Pallas kernels: none -> 13.3 us  [factor(): pl.pallas_call(eliminate, out_shape=jax.ShapeDtypeStruct((PW, 2 * PW), F3...]
    all_to_all x1, waiting for transfers between devices: 0.01 us -> 5.36 us  [body(): sent = lax.all_to_all(sent, 'rows', 0, 0, tiled=True)]
    all_to_all x2, waiting for transfers between devices: 29 us -> 34.3 us  [spread(): lax.all_to_all(jnp.broadcast_to(value[None], (size,) + value.shape), axis...]
    dot_general x17 -> x18, matrix products: 15.1 us -> 18.7 us  [mm(): lax.dot_general(left, right, ((contract[0], contract[1]), ((), ())), prec...]
    unnamed x11 -> x9, local copies, waits for them, and re-layouts: 2.6 us -> 0.02 us
    all_to_all x2, starting transfers between devices: 11.5 us -> 9.2 us  [spread(): lax.all_to_all(jnp.broadcast_to(value[None], (size,) + value.shape), axis...]
    convert_element_type x0 -> x2, other arithmetic: none -> 1.49 us  [the longest x1 1.49 us: body(): sent.reshape(wide + 16, owners, part).transpose(1, 0, 2)]
  transfers between devices with their start and end apart: 4 -> 4, of which waited for: 3 -> 4; matrix products, arithmetic and copies ran while one was open for 31% -> 10% of each run, Pallas kernels for 0% -> 11%
where the time goes in v2:
time: 128 us; the launch traced here: 126 us
  waiting for transfers between devices  50.1 us (39%)
  starting transfers between devices  21.1 us (16%)
  matrix products  18.7 us (15%)
  Pallas kernels  13.3 us (10%)
  other arithmetic  9.8 us (8%)
  blocking collectives  6.4 us (5%)
  local copies, waits for them, and re-layouts  4.16 us (3%)
  between operations  2.91 us (2%)
    all_to_all x2, waiting for transfers between devices, spread(): lax.all_to_all(jnp.broadcast_to(value[None], (size,) + value.shape), axis...  34.3 us
    dot_general x18, matrix products, mm(): lax.dot_general(left, right, ((contract[0], contract[1]), ((), ())), prec...  18.7 us
    pallas_call x2, Pallas kernels, factor(): pl.pallas_call(eliminate, out_shape=jax.ShapeDtypeStruct((PW, 2 * PW), F3...  13.3 us
    all_to_all x1, waiting for transfers between devices, body(): arrived = lax.all_to_all(payload, 'rows', 0, 0, tiled=True)  10.5 us
    all_to_all x2, starting transfers between devices, spread(): lax.all_to_all(jnp.broadcast_to(value[None], (size,) + value.shape), axis...  9.2 us
    all_to_all x1, starting transfers between devices, body(): arrived = lax.all_to_all(payload, 'rows', 0, 0, tiled=True)  7.36 us
    all_to_all x1, waiting for transfers between devices, body(): sent = lax.all_to_all(sent, 'rows', 0, 0, tiled=True)  5.36 us
    all_to_all x1, starting transfers between devices, body(): sent = lax.all_to_all(sent, 'rows', 0, 0, tiled=True)  4.56 us
  transfers between devices with their start and end apart: 4, of which 4 were waited for; matrix products, arithmetic and copies ran while one was open for 10% of the time, Pallas kernels for 11%

profile of v2, /device:TPU:8, one launch (start us, length us, event | category | flops | bytes accessed | tf_op | source)
XLA Modules:
  0.0 126.5 jit_solution(6023000841175419896)
XLA Ops:
  0.6 0.0 slice-start
  0.6 0.0 copy-start.2
  0.7 0.7 dynamic-slice_bitcast_fusion
  1.4 0.2 convert_reduce_fusion.1
  1.5 0.7 multiply_add_fusion
  2.2 0.8 dynamic-slice_add_fusion
  3.0 0.1 select_convert_fusion
  3.1 1.2 convolution_convert_fusion.1
  4.3 0.9 all_to_all.17
  5.2 7.4 %all-to-all-start = ((bf16[16,12,1152]{2,1,0:T(8,128)(2,1)}), bf16[16,12,1152]{2,1,0:T(8,128)(2,1)S(1)}, u32[]{:S(2)}, u32[]{:S(2)}) async-start(bf16[16,12,1152]{2,1,0:T(8,128)(2,1)} %all_to_all.17), calls=%async_computation | async-start | bytes 1179648 | tf_op jit(solution)/shard_map/all_to_all | solution.py:94
  12.6 0.1 pad.12.clone
  12.6 0.0 copy-done.2
  12.6 1.8 %all-gather.2 = f32[2,1,128]{2,1,0:T(1,128)S(1)} all-gather(f32[1,1,128]{2,1,0:T(1,128)S(1)} %slice_bitcast_fusion.1), channel_id=2, replica_groups=mesh['rows'=16,'cols'=2] {'cols'}, dimensions={0}, use_global_device_ids=true | all-gather | bytes 1536 | tf_op jit(solution)/shard_map/all_gather | solution.py:26
  14.4 0.6 multiply_reduce_fusion.1
  15.0 0.0 slice-done
  15.0 2.2 %all-gather.1 = bf16[256,1024]{1,0:T(8,128)(2,1)S(1)} all-gather(bf16[128,1024]{1,0:T(8,128)(2,1)S(1)} %slice-done), channel_id=3, replica_groups=mesh['rows'=16,'cols'=2] {'cols'}, dimensions={0}, use_global_device_ids=true | all-gather | bytes 786432 | tf_op jit(solution)/shard_map/all_gather | solution.py:26
  17.2 0.6 broadcast_divide_fusion
  17.9 10.5 %all-to-all-done = bf16[16,12,1152]{2,1,0:T(8,128)(2,1)S(1)} async-done(((bf16[16,12,1152]{2,1,0:T(8,128)(2,1)}), bf16[16,12,1152]{2,1,0:T(8,128)(2,1)S(1)}, u32[]{:S(2)}, u32[]{:S(2)}) %all-to-all-start) | async-done | bytes 442400 | tf_op jit(solution)/shard_map/all_to_all | solution.py:94
  28.4 0.1 all_to_all.19
  28.5 2.4 %all_gather.15 = bf16[384,1152]{1,0:T(8,128)(2,1)S(1)} all-gather(bf16[192,1152]{1,0:T(8,128)(2,1)S(1)} %all_to_all.19), channel_id=1, replica_groups=mesh['rows'=16,'cols'=2] {'cols'}, dimensions={0}, use_global_device_ids=true | all-gather | bytes 1327104 | tf_op jit(solution)/shard_map/all_gather | solution.py:95
  30.9 0.1 add_reduce_fusion
  31.1 0.0 copy-done.3
  31.1 6.5 %convolution_multiply_fusion = f32[64,4096]{1,0:T(8,128)S(1)} fusion(bf16[4096,1024]{1,0:T(8,128)(2,1)} %param.8, f32[4096]{0:T(1024)S(1)} %copy-done.2, bf16[384,1152]{1,0:T(8,128)(2,1)S(1)} %all_gather.15, f32[64]{0:T(128)S(1)} %copy-done.3, s32[384]{0:T(512)S(1)} %add_reduce_fusion), kind=kOutput, calls=%fused_computation.4 | convolution fusion | flops 3430703104 | bytes 10242560 | tf_op jit(solution)/shard_map/dot_general | solution.py:19
  37.6 0.6 multiply_reduce_fusion
  38.2 0.9 broadcast_in_dim.21
  39.1 4.6 %all-to-all-start.1 = ((f32[16,64,128]{2,1,0:T(8,128)}), f32[16,64,128]{2,1,0:T(8,128)S(1)}, u32[]{:S(2)}, u32[]{:S(2)}) async-start(f32[16,64,128]{2,1,0:T(8,128)} %broadcast_in_dim.21), calls=%async_computation.1 | async-start | bytes 1048576 | tf_op jit(solution)/shard_map/all_to_all | solution.py:37
  43.7 1.9 %convolution_convert_fusion = bf16[128,4096]{1,0:T(8,128)(2,1)S(1)} fusion(f32[64,4096]{1,0:T(8,128)S(1)} %convolution_multiply_fusion, f32[64,128]{1,0:T(8,128)S(1)} %get-tuple-element.5, f32[128]{0:T(128)S(1)} %slice_bitcast_fusion, f32[64]{0:T(128)S(1)} %get-tuple-element.4), kind=kOutput, calls=%fused_computation.2 | convolution fusion | flops 403193856 | bytes 2130688 | tf_op jit(solution)/shard_map/dot_general | solution.py:19
  45.6 0.1 copy.22
  45.7 0.6 fusion.45
  46.3 1.5 %maximum_bitcast_fusion = bf16[16,144,256]{2,1,0:T(8,128)(2,1)} fusion(bf16[1,16,256]{2,0,1:T(2,128)(2,1)S(1)} %concatenate.61, bf16[1,16,256]{2,0,1:T(2,128)(2,1)S(1)} %concatenate.60, bf16[128,16,256]{2,0,1:T(8,128)(2,1)S(1)} %bitcast.53, bf16[144]{0:T(256)(128)(2,1)S(1)} %pad.12.clone), kind=kLoop, calls=%fused_computation.8 | loop fusion | flops 4718592 | bytes 2244896 | tf_op jit(solution)/shard_map/convert_element_type | solution.py:119
  47.8 10.6 %all-to-all-done.1 = f32[16,64,128]{2,1,0:T(8,128)S(1)} async-done(((f32[16,64,128]{2,1,0:T(8,128)}), f32[16,64,128]{2,1,0:T(8,128)S(1)}, u32[]{:S(2)}, u32[]{:S(2)}) %all-to-all-start.1) | async-done | bytes 524320 | tf_op jit(solution)/shard_map/all_to_all | solution.py:37
  58.4 4.6 %all-to-all-start.2 = ((bf16[16,144,256]{2,1,0:T(8,128)(2,1)}), bf16[16,144,256]{2,1,0:T(8,128)(2,1)S(1)}, u32[]{:S(2)}, u32[]{:S(2)}) async-start(bf16[16,144,256]{2,1,0:T(8,128)(2,1)} %maximum_bitcast_fusion), calls=%async_computation.2 | async-start | bytes 2359296 | tf_op jit(solution)/shard_map/all_to_all | solution.py:120
  63.7 1.0 convolution_bitcast_fusion
  64.7 0.6 select_reduce_fusion.1
  66.0 0.7 pad_maximum_fusion.2.in_ref
  66.7 6.6 %shard_map.86 = f32[64,128]{1,0:T(8,128)} custom-call(f32[64,128]{1,0:T(8,128)} %pad_maximum_fusion.2.in_ref), custom_call_target="tpu_custom_call" | custom-call | flops 8000000 | bytes 65536 | tf_op jit(solution)/shard_map/pallas_call | solution.py:56
  73.3 1.1 fusion.27
  74.4 1.0 fusion.35
  75.4 1.0 convolution_subtract_fusion.4
  76.4 0.2 fusion.56
  76.6 0.8 select_reduce_fusion
  78.1 0.7 pad_maximum_fusion.3.in_ref
  78.8 6.6 %shard_map.87 = f32[64,128]{1,0:T(8,128)} custom-call(f32[64,128]{1,0:T(8,128)} %pad_maximum_fusion.3.in_ref), custom_call_target="tpu_custom_call" | custom-call | flops 8000000 | bytes 65536 | tf_op jit(solution)/shard_map/pallas_call | solution.py:56
  85.4 5.4 %all-to-all-done.2 = bf16[16,144,256]{2,1,0:T(8,128)(2,1)S(1)} async-done(((bf16[16,144,256]{2,1,0:T(8,128)(2,1)}), bf16[16,144,256]{2,1,0:T(8,128)(2,1)S(1)}, u32[]{:S(2)}, u32[]{:S(2)}) %all-to-all-start.2) | async-done | bytes 1179680 | tf_op jit(solution)/shard_map/all_to_all | solution.py:120
  90.8 0.2 convert_reduce_fusion
  90.9 0.1 slice_add_fusion
  91.0 0.3 fusion.55
  91.3 0.2 convolution_subtract_fusion.1
  91.5 1.0 convolution_convert_fusion.2
  92.6 1.1 broadcast_in_dim.24
  93.6 4.6 %all-to-all-start.3 = ((bf16[16,128,256]{2,1,0:T(8,128)(2,1)}), bf16[16,128,256]{2,1,0:T(8,128)(2,1)S(1)}, u32[]{:S(2)}, u32[]{:S(2)}) async-start(bf16[16,128,256]{2,1,0:T(8,128)(2,1)} %broadcast_in_dim.24), calls=%async_computation.3 | async-start | bytes 2097152 | tf_op jit(solution)/shard_map/all_to_all | solution.py:37
  98.2 0.3 fusion.25
  98.5 0.2 convolution_subtract_fusion.2
  98.7 0.3 fusion.32
  98.9 23.6 %all-to-all-done.3 = bf16[16,128,256]{2,1,0:T(8,128)(2,1)S(1)} async-done(((bf16[16,128,256]{2,1,0:T(8,128)(2,1)}), bf16[16,128,256]{2,1,0:T(8,128)(2,1)S(1)}, u32[]{:S(2)}, u32[]{:S(2)}) %all-to-all-start.3) | async-done | bytes 1048608 | tf_op jit(solution)/shard_map/all_to_all | solution.py:37
  122.6 0.1 copy.20
  122.7 0.2 convert_element_type.56
  122.9 0.1 slice.117
  123.0 0.6 convolution_subtract_fusion
  123.7 0.1 slice.121
  123.7 0.1 slice_select_fusion.1
  123.8 1.0 pad_maximum_fusion
  124.9 0.1 slice_select_fusion
  124.9 1.5 %maximum_multiply_fusion = f32[128,4096]{1,0:T(8,128)} fusion(f32[128,3968]{1,0:T(8,128)S(1)} %slice.117, f32[128,128]{1,0:T(8,128)S(1)} %slice_select_fusion), kind=kLoop, calls=%fused_computation.7 | loop fusion | flops 1048576 | bytes 4194304 | tf_op jit(solution)/shard_map/mul | solution.py:151
  (17 shorter events, 0.1 us)
Async XLA Ops:
  0.6 14.4 %slice-start = ((bf16[4096,1024]{1,0:T(8,128)(2,1)}), bf16[128,1024]{1,0:T(8,128)(2,1)S(1)}, s32[]{:S(2)}) async-start(bf16[4096,1024]{1,0:T(8,128)(2,1)} %param.8), calls=%async_computation.4 | async-start | bytes 524288 | tf_op jit(solution)/shard_map/slice | solution.py:75
  0.6 12.0 %copy-start.2 = (f32[4096]{0:T(1024)S(1)}, f32[4096]{0:T(1024)}, u32[]{:S(2)}) copy-start(f32[4096]{0:T(1024)} %param.9) | copy-start | bytes 49156
  5.2 25.9 %copy-start.3 = (f32[64]{0:T(128)S(1)}, f32[64]{0:T(128)}, u32[]{:S(2)}) copy-start(f32[64]{0:T(128)} %param.12) | copy-start | bytes 772
  5.2 23.2 %all-to-all-start = ((bf16[16,12,1152]{2,1,0:T(8,128)(2,1)}), bf16[16,12,1152]{2,1,0:T(8,128)(2,1)S(1)}, u32[]{:S(2)}, u32[]{:S(2)}) async-start(bf16[16,12,1152]{2,1,0:T(8,128)(2,1)} %all_to_all.17), calls=%async_computation | async-start | bytes 1179648 | tf_op jit(solution)/shard_map/all_to_all | solution.py:94
  39.1 19.4 %all-to-all-start.1 = ((f32[16,64,128]{2,1,0:T(8,128)}), f32[16,64,128]{2,1,0:T(8,128)S(1)}, u32[]{:S(2)}, u32[]{:S(2)}) async-start(f32[16,64,128]{2,1,0:T(8,128)} %broadcast_in_dim.21), calls=%async_computation.1 | async-start | bytes 1048576 | tf_op jit(solution)/shard_map/all_to_all | solution.py:37
  58.4 32.3 %all-to-all-start.2 = ((bf16[16,144,256]{2,1,0:T(8,128)(2,1)}), bf16[16,144,256]{2,1,0:T(8,128)(2,1)S(1)}, u32[]{:S(2)}, u32[]{:S(2)}) async-start(bf16[16,144,256]{2,1,0:T(8,128)(2,1)} %maximum_bitcast_fusion), calls=%async_computation.2 | async-start | bytes 2359296 | tf_op jit(solution)/shard_map/all_to_all | solution.py:120
  73.3 17.7 %copy-start = (f32[64,128]{1,0:T(8,128)S(1)}, f32[64,128]{1,0:T(8,128)}, u32[]{:S(2)}) copy-start(f32[64,128]{1,0:T(8,128)} %shard_map.86) | copy-start | bytes 98308
  90.9 7.7 %copy-start.1 = (f32[64,128]{1,0:T(8,128)S(1)}, f32[64,128]{1,0:T(8,128)}, u32[]{:S(2)}) copy-start(f32[64,128]{1,0:T(8,128)} %shard_map.87) | copy-start | bytes 98308
  93.6 28.9 %all-to-all-start.3 = ((bf16[16,128,256]{2,1,0:T(8,128)(2,1)}), bf16[16,128,256]{2,1,0:T(8,128)(2,1)S(1)}, u32[]{:S(2)}, u32[]{:S(2)}) async-start(bf16[16,128,256]{2,1,0:T(8,128)(2,1)} %broadcast_in_dim.24), calls=%async_computation.3 | async-start | bytes 2097152 | tf_op jit(solution)/shard_map/all_to_all | solution.py:37
